TPU v7x, 32 devices: a whole 2x2x4 slice. The times are simulated.
32 devices in a mesh: row: 8 (over y, x, core), ctx: 4 (over z).
Axes of the slice: x: 2, y: 2, z: 4, core: 2. Of those that a mesh axis runs over, the one named last changes fastest.
Arguments:
- queries: bfloat16 [5, 4096, 128], P(None, ('row', 'ctx')), may hold values from -100 to 100
- keys: bfloat16 [4096, 128], P('ctx'), may hold values from -6 to 6
- doc_ids: int32 [64], replicated, may hold values from 0 to 3, never falling along the last dimension, each value on 1 to 48 neighbouring positions
- gate_query: bfloat16 [5, 128, 128], replicated, may hold values from -0.5 to 0.5
- gate_key: bfloat16 [384, 128], replicated, may hold values from -0.3125 to 0.3125
Outputs:
- block_map: float32 [5, 64, 64], P(None, ('row', 'ctx'))
- grad_query: float32 [5, 128, 128], replicated
- grad_key: float32 [384, 128], replicated
Inputs may be any that keep to these rules, and one draw needn't show every extreme that they name: `doc_ids`: block document ids never fall along the sequence; each document spans 1 to 48 blocks and one spans exactly 48.
All inputs are finite; a program needn't handle non-finite values.
Results may differ from a plain program's by a relative error of at most 0.0003.
Values may be sent and summed in bfloat16 or wider, within the bound.
A program may use at most 64 MiB of HBM per device.

v0:
```python
import math
import jax
import jax.numpy as jnp
from jax import lax
from jax.sharding import PartitionSpec as P

BLK = 64
NEG_FILL = -1e30
BLOCK_CAP = 512


def pool_keys(key_block, block_len):
    grouped = key_block.astype(jnp.float32).reshape(
        key_block.shape[0] // block_len, block_len, key_block.shape[1]
    )
    return jnp.concatenate(
        [jnp.max(grouped, axis=1), jnp.min(grouped, axis=1), jnp.mean(grouped, axis=1)], axis=1
    )


def held_positions(row_index, ctx_index, ctx_total, row_count):
    half_rows = row_count // 2
    home_start = (row_index * ctx_total + ctx_index) * row_count
    far_start = home_start + half_rows
    offsets = jnp.arange(half_rows, dtype=jnp.int32)
    return jnp.concatenate([home_start + offsets, far_start + offsets])


def block_docs(doc_ids, positions, block_len):
    block_starts = positions.reshape(-1, block_len)[:, 0] // block_len
    return jnp.repeat(jnp.take(doc_ids, block_starts), block_len)


def tile_update(
    carried,
    held_rows,
    query_pos,
    query_doc,
    key_block,
    key_start,
    table_base,
    doc_ids,
    block_len,
    score_scale,
):
    score_table, row_max, row_sum = carried
    key_count = key_block.shape[0]
    head_count, row_count = (held_rows.shape[0], held_rows.shape[1])
    scores = (
        jnp.einsum("hrd,kd->hrk", held_rows, key_block, preferred_element_type=jnp.float32)
        * score_scale
    )
    key_pos = key_start + jnp.arange(key_count, dtype=jnp.int32)
    key_doc = jnp.repeat(
        lax.dynamic_slice_in_dim(doc_ids, key_start // block_len, key_count // block_len), block_len
    )
    allowed = (key_pos[None, :] <= query_pos[:, None]) & (key_doc[None, :] == query_doc[:, None])
    masked = jnp.where(allowed[None], scores, NEG_FILL)
    block_peaks = jnp.max(
        masked.reshape(head_count, row_count, key_count // block_len, block_len), axis=3
    )
    score_table = lax.dynamic_update_slice_in_dim(
        score_table, block_peaks, (key_start - table_base) // block_len, 2
    )
    new_max = jnp.maximum(row_max, jnp.max(masked, axis=2))
    weights = jnp.where(allowed[None], jnp.exp(masked - new_max[:, :, None]), 0.0)
    row_sum = row_sum * jnp.exp(row_max - new_max) + jnp.sum(weights, axis=2)
    return (score_table, new_max, row_sum)


def finish_maps(score_table, row_max, row_sum, block_len):
    log_total = row_max + jnp.log(row_sum)
    chances = jnp.exp(score_table - log_total[:, :, None])
    head_count, row_count, column_count = chances.shape
    return jnp.max(
        chances.reshape(head_count, row_count // block_len, block_len, column_count), axis=2
    )


def key_pass(
    held_rows, query_pos, query_doc, key_shard, doc_ids, block_len, score_scale, total_blocks
):
    head_count, row_count, head_dim = held_rows.shape
    query_top = jnp.max(query_pos)
    doc_floor = jnp.min(query_doc)
    initial = (
        jnp.full((head_count, row_count, total_blocks), NEG_FILL, jnp.float32),
        jnp.full((head_count, row_count), NEG_FILL, jnp.float32),
        jnp.zeros((head_count, row_count), jnp.float32),
        jnp.zeros((total_blocks, 3 * head_dim), jnp.float32),
    )
    key_piece = lax.all_gather(key_shard, "ctx", axis=0, tiled=True)
    piece_rows = key_piece.shape[0]
    sub_rows = math.gcd(piece_rows, BLOCK_CAP)

    def advance(turn_index, inner):
        stats = inner[:3]
        pooled = inner[3]
        key_start = turn_index * sub_rows
        key_block = lax.dynamic_slice_in_dim(key_piece, turn_index * sub_rows, sub_rows, 0)
        pooled = lax.dynamic_update_slice_in_dim(
            pooled, pool_keys(key_block, block_len), key_start // block_len, 0
        )

        def sweep(current):
            return tile_update(
                current,
                held_rows,
                query_pos,
                query_doc,
                key_block,
                key_start,
                0,
                doc_ids,
                block_len,
                score_scale,
            )

        def keep_stats(current):
            return current

        last_doc = lax.dynamic_index_in_dim(
            doc_ids, (key_start + sub_rows - 1) // block_len, 0, keepdims=False
        )
        needed = (key_start <= query_top) & (last_doc >= doc_floor)
        stats = lax.cond(needed, sweep, keep_stats, stats)
        return stats + (pooled,)

    score_table, row_max, row_sum, pooled = lax.fori_loop(
        0, piece_rows // sub_rows, advance, initial
    )
    return (finish_maps(score_table, row_max, row_sum, block_len), pooled)


def gate_gradients(query_pool, pooled, gate_query, gate_key, block_map, block_allowed):
    query_gate = jnp.einsum(
        "hbd,hde->hbe", query_pool, gate_query.astype(jnp.float32), precision=lax.Precision.HIGHEST
    )
    key_gate = jnp.dot(pooled, gate_key.astype(jnp.float32), precision=lax.Precision.HIGHEST)
    gate_logits = jnp.einsum("hbe,ke->hbk", query_gate, key_gate, precision=lax.Precision.HIGHEST)
    gate_exp = jnp.where(block_allowed[None], jnp.exp(gate_logits), 0.0)
    gate_prob = gate_exp / jnp.sum(gate_exp, axis=2, keepdims=True)
    target = block_map / jnp.sum(block_map, axis=2, keepdims=True)
    diff = gate_prob - target
    query_back = jnp.einsum("hbk,ke->hbe", diff, key_gate, precision=lax.Precision.HIGHEST)
    query_term = jnp.einsum("hbd,hbe->hde", query_pool, query_back, precision=lax.Precision.HIGHEST)
    key_back = jnp.einsum("hbk,hbe->ke", diff, query_gate, precision=lax.Precision.HIGHEST)
    key_term = jnp.dot(pooled.T, key_back, precision=lax.Precision.HIGHEST)
    return (query_term, key_term)


def shards(queries, keys, doc_ids, gate_query, gate_key):
    head_count, row_count, head_dim = queries.shape
    block_len = BLK
    total_blocks = doc_ids.shape[0]
    score_scale = 1.0 / math.sqrt(head_dim)
    ctx_total = lax.axis_size("ctx")
    row_index = lax.axis_index("row")
    ctx_index = lax.axis_index("ctx")
    query_pos = held_positions(row_index, ctx_index, ctx_total, row_count)
    query_doc = block_docs(doc_ids, query_pos, block_len)
    held_maps, pooled = key_pass(
        queries, query_pos, query_doc, keys, doc_ids, block_len, score_scale, total_blocks
    )
    home_count = row_count // block_len
    home_blocks = (row_index * ctx_total + ctx_index) * home_count + jnp.arange(
        home_count, dtype=jnp.int32
    )
    home_docs = jnp.take(doc_ids, home_blocks)
    all_blocks = jnp.arange(total_blocks, dtype=jnp.int32)
    block_allowed = (all_blocks[None, :] <= home_blocks[:, None]) & (
        doc_ids[None, :] == home_docs[:, None]
    )
    query_pool = jnp.mean(
        queries.astype(jnp.float32).reshape(head_count, home_count, block_len, head_dim), axis=2
    )
    query_term, key_term = gate_gradients(
        query_pool, pooled, gate_query, gate_key, held_maps, block_allowed
    )
    grad_query, grad_key = lax.psum((query_term, key_term), ("row", "ctx"))
    return (held_maps, grad_query, grad_key)


def solution(mesh):
    in_specs = (P(None, ("row", "ctx"), None), P("ctx", None), P(), P(), P())
    out_specs = (P(None, ("row", "ctx"), None), P(), P())
    return jax.shard_map(shards, mesh=mesh, in_specs=in_specs, out_specs=out_specs, check_vma=False)
```

profile of v0, /device:TPU:0, one launch (start us, length us, event | category | flops | bytes accessed | tf_op | source)
XLA Modules:
  0.0 220.2 jit_solution(13385890775669702233)
XLA Ops:
  7.2 0.7 all-gather.2.cloned.1.call-update
  8.3 1.3 gather_fusion
  9.6 1.3 gather_fusion.1
  10.9 0.6 fusion.18
  12.9 0.7 broadcast_reduce_fusion
  13.7 0.2 fusion.12
  14.0 26.4 %all-gather.2.cloned.1.call-done = bf16[4096,128]{1,0:T(8,128)(2,1)} async-done(((bf16[1024,128]{1,0:T(8,128)(2,1)}), bf16[4096,128]{1,0:T(8,128)(2,1)}) %all-gather.2.cloned.1.call-update) | async-done | bytes 1048592 | tf_op jit(solution)/shard_map/all_gather | solution.py:92
  40.4 27.2 %while.25 = (s32[]{:T(128)}, f32[5,128,64]{1,2,0:T(8,128)S(1)}, f32[5,128]{1,0:T(8,128)S(1)}, f32[5,128]{1,0:T(8,128)S(1)}, f32[64,384]{1,0:T(8,128)S(1)}, /*ind...) while((s32[]{:T(128)}, f32[5,128,64]{1,2,0:T(8,128)S(1)}, ...), condition=%wide.region_12.14_spmd.clone, body=%wide.region_3.13_spmd.clone.sunk | while | flops 86640432 | bytes 7622712 | solution.py:129
  40.4 1.0 bitcast_reduce_fusion.4
  41.5 0.2 dynamic_update_slice.19
  41.7 0.6 dynamic_slice.37
  43.6 2.2 conditional.3
  44.1 0.4 fusion.23
  44.6 0.4 select_reduce_fusion
  45.0 0.4 copy.26
  45.4 0.2 bitcast_reduce_fusion
  45.8 0.9 bitcast_reduce_fusion.4
  46.8 0.2 dynamic_update_slice.19
  47.0 0.6 dynamic_slice.37
  48.9 0.9 bitcast_reduce_fusion.4
  49.9 0.2 dynamic_update_slice.19
  50.2 0.6 dynamic_slice.37
  52.0 0.9 bitcast_reduce_fusion.4
  53.1 0.2 dynamic_update_slice.19
  53.3 0.6 dynamic_slice.37
  55.1 0.9 bitcast_reduce_fusion.4
  56.2 0.2 dynamic_update_slice.19
  56.4 0.6 dynamic_slice.37
  58.3 0.9 bitcast_reduce_fusion.4
  59.3 0.2 dynamic_update_slice.19
  59.5 0.6 dynamic_slice.37
  61.4 0.9 bitcast_reduce_fusion.4
  62.5 0.2 dynamic_update_slice.19
  62.7 0.6 dynamic_slice.37
  64.5 0.9 bitcast_reduce_fusion.4
  65.6 0.1 dynamic_update_slice.19
  65.8 0.6 dynamic_slice.37
  67.7 0.2 copy.33
  68.1 0.2 convolution_bitcast_fusion.1
  68.3 0.2 fusion.4
  68.4 0.2 fusion.10
  68.6 0.3 convolution_bitcast_fusion
  69.0 0.2 fusion.21
  69.2 1.2 fusion.24
  70.4 1.4 fusion.8
  71.8 138.2 %all-reduce.3.cloned.1.call-done = (f32[5,128,128]{2,1,0:T(8,128)}, f32[384,128]{1,0:T(8,128)}) async-done(((f32[5,128,128]{2,1,0:T(8,128)}, f32[384,128]{1,0:T(8,128)}), (f32[5,128,128]{2,1,0:T(8,128)}, f32[384,128]{1,0:T(8,128)})) %all-reduce.3.cloned.1.call-update) | async-done | bytes 524304 | tf_op jit(solution)/shard_map/psum | solution.py:180
  210.1 1.7 copy.70
  211.8 1.6 copy.71
  (84 shorter events, 2.1 us)
Async XLA Ops:
  7.2 6.6 %copy-start = (bf16[5,128,128]{2,1,0:T(8,128)(2,1)S(1)}, bf16[5,128,128]{2,1,0:T(8,128)(2,1)}, u32[]{:S(2)}) copy-start(bf16[5,128,128]{2,1,0:T(8,128)(2,1)} %param.14) | copy-start | bytes 491524
  7.2 6.5 %copy-start.1 = (s32[64]{0:T(128)S(1)}, s32[64]{0:T(128)}, u32[]{:S(2)}) copy-start(s32[64]{0:T(128)} %param.13) | copy-start | bytes 772
  7.2 6.4 %copy-start.2 = (bf16[5,128,128]{2,1,0:T(8,128)(2,1)S(1)}, bf16[5,128,128]{2,1,0:T(8,128)(2,1)}, u32[]{:S(2)}) copy-start(bf16[5,128,128]{2,1,0:T(8,128)(2,1)} %param.11) | copy-start | bytes 491524
  7.2 33.2 %all-gather.2.cloned.1.call-start = ((), (), s32[]{:S(2)}) async-start(), calls=%async_computation | async-start | bytes 1310720 | tf_op jit(solution)/shard_map/all_gather | solution.py:92
  7.9 202.1 %all-reduce.3.cloned.1.call-start = ((), (), s32[]{:S(2)}) async-start(), calls=%async_computation.1 | async-start | bytes 1048576 | tf_op jit(solution)/shard_map/psum | solution.py:180
  40.4 27.7 %copy-start.3 = (bf16[384,128]{1,0:T(8,128)(2,1)S(1)}, bf16[384,128]{1,0:T(8,128)(2,1)}, u32[]{:S(2)}) copy-start(bf16[384,128]{1,0:T(8,128)(2,1)} %param.15) | copy-start | bytes 294916
  67.9 145.5 %copy-start.4 = (f32[5,2,64]{2,1,0:T(2,128)}, f32[5,2,64]{2,1,0:T(2,128)S(1)}, u32[]{:S(2)}) copy-start(f32[5,2,64]{2,1,0:T(2,128)S(1)} %bitcast_reduce_fusion.2) | copy-start | bytes 7684
Sparse Core Ops, SparseCore 0:
  9.6 30.7 all-gather.1
  71.9 138.0 all-reduce.2
where the time goes:
time: 221 us; the launch traced here: 220 us
  waiting for transfers between devices  165 us (75%)
  between operations  15.5 us (7%)
  local copies, waits for them, and re-layouts  13.4 us (6%)
  loops' own time  11 us (5%)
  other arithmetic  10.7 us (5%)
  matrix products  4.21 us (2%)
    psum x1, waiting for transfers between devices, shards(): grad_query, grad_key = lax.psum((query_term, key_term), ('row', 'ctx'))  138 us
    all_gather x1, waiting for transfers between devices, key_pass(): key_piece = lax.all_gather(key_shard, 'ctx', axis=0, tiled=True)  26.4 us
    another operation x1, loops' own time, key_pass(): lax.fori_loop(0, piece_rows // sub_rows, advance, initial)  10.8 us
    reduce_max x16, other arithmetic, pool_keys(): jnp.max(grouped, axis=1)  7.65 us
    dynamic_slice x8, local copies, waits for them, and re-layouts, advance(): lax.dynamic_index_in_dim(doc_ids, (key_start + sub_rows - 1) // block_len...  4.69 us
  transfers between devices with their start and end apart: 2, of which 2 were waited for; matrix products, arithmetic and copies ran while one was open for 2% of the time, Pallas kernels for 0%

commit v1 on v0

--- a/solution.py
+++ b/solution.py
@@ -7,6 +7,12 @@
 BLK = 64
 NEG_FILL = -1e30
 BLOCK_CAP = 512
+
+
+def laid_out(tiles, dim):
+    tiles = jnp.moveaxis(tiles, 0, dim)
+    shape = tiles.shape
+    return tiles.reshape(*shape[:dim], shape[dim] * shape[dim + 1], *shape[dim + 2 :])
 
 
 def pool_keys(key_block, block_len):
@@ -89,7 +95,19 @@
         jnp.zeros((head_count, row_count), jnp.float32),
         jnp.zeros((total_blocks, 3 * head_dim), jnp.float32),
     )
-    key_piece = lax.all_gather(key_shard, "ctx", axis=0, tiled=True)
+    peers = lax.axis_size("ctx")
+    pairs = [(i, (i + 1) % peers) for i in range(peers)]
+    back = [(b, a) for a, b in pairs]
+    lower, upper = ([], [])
+    for step in range(peers - 1):
+        if step % 2 == 0:
+            lower.append(lax.ppermute(lower[-1] if lower else key_shard, "ctx", pairs))
+        else:
+            upper.append(lax.ppermute(upper[-1] if upper else key_shard, "ctx", back))
+    tiles = jnp.stack([*lower[::-1], key_shard, *upper])
+    shift = lax.axis_index("ctx") - len(lower)
+    tiles = tiles[(jnp.arange(peers) - shift) % peers]
+    key_piece = laid_out(tiles, 0)
     piece_rows = key_piece.shape[0]
     sub_rows = math.gcd(piece_rows, BLOCK_CAP)
 

time: 221 us -> 211 us (0.955)
  waiting for transfers between devices: 165 us -> 147 us
  starting transfers between devices: 0.08 us -> 5.24 us
    all_gather x1 -> x0, waiting for transfers between devices: 26.4 us -> none  [key_pass(): key_piece = lax.all_gather(key_shard, 'ctx', axis=0, tiled=True)]
    ppermute x0 -> x3, waiting for transfers between devices: none -> 10.1 us  [the longest x2 7.9 us: key_pass(): lower.append(lax.ppermute(lower[-1] if lower else key_shard, 'ctx', pairs))]
    ppermute x0 -> x3, starting transfers between devices: none -> 5.2 us  [the longest x2 3.11 us: key_pass(): lower.append(lax.ppermute(lower[-1] if lower else key_shard, 'ctx', pairs))]
  transfers between devices with their start and end apart: 2 -> 4, of which waited for: 2 -> 4; matrix products, arithmetic and copies ran while one was open for 2% -> 3% of each run, Pallas kernels for 0% -> 0%
where the time goes in v1:
time: 211 us; the launch traced here: 210 us
  waiting for transfers between devices  147 us (70%)
  between operations  15.5 us (7%)
  local copies, waits for them, and re-layouts  15.1 us (7%)
  other arithmetic  12.5 us (6%)
  loops' own time  11.3 us (5%)
  starting transfers between devices  5.24 us (2%)
  matrix products  4.21 us (2%)
    psum x1, waiting for transfers between devices, shards(): grad_query, grad_key = lax.psum((query_term, key_term), ('row', 'ctx'))  136 us
    another operation x1, loops' own time, key_pass(): lax.fori_loop(0, piece_rows // sub_rows, advance, initial)  11.1 us
    ppermute x2, waiting for transfers between devices, key_pass(): lower.append(lax.ppermute(lower[-1] if lower else key_shard, 'ctx', pairs))  7.9 us
    reduce_max x16, other arithmetic, pool_keys(): jnp.max(grouped, axis=1)  7.65 us
    dynamic_slice x8, local copies, waits for them, and re-layouts, advance(): lax.dynamic_index_in_dim(doc_ids, (key_start + sub_rows - 1) // block_len...  4.69 us
  transfers between devices with their start and end apart: 4, of which 4 were waited for; matrix products, arithmetic and copies ran while one was open for 3% of the time, Pallas kernels for 0%

profile of v1, /device:TPU:0, one launch (start us, length us, event | category | flops | bytes accessed | tf_op | source)
XLA Modules:
  0.0 210.5 jit_solution(4041804967353970041)
XLA Ops:
  7.2 3.1 %collective-permute-start = (bf16[1024,128]{1,0:T(8,128)(2,1)}, bf16[1024,128]{1,0:T(8,128)(2,1)S(1)}, u32[]{:S(2)}, u32[]{:S(2)}) collective-permute-start(bf16[1024,128]{1,0:T(8,128)(2,1)} %param.12), channel_id=1, source_target_pairs={{0,1},{1,2},{2,3},{3,0},{4,5},{5,6},{6,7},{7,4},{8,9},{9,10},{10,1... | collective-permute-start | bytes 786440 | tf_op jit(solution)/shard_map/ppermute | solution.py:104
  10.3 2.1 collective-permute-start.2
  12.7 1.3 gather_fusion.1
  14.1 0.8 broadcast_reduce_fusion
  14.8 1.3 gather_fusion.2
  16.2 1.0 convert_reduce_fusion.2
  17.1 0.7 compare_and_fusion.1
  17.9 1.9 collective-permute-done
  19.8 0.6 fusion.20
  21.7 0.2 fusion.12
  22.0 2.2 %collective-permute-done.2 = bf16[1024,128]{1,0:T(8,128)(2,1)S(1)} collective-permute-done((bf16[1024,128]{1,0:T(8,128)(2,1)}, bf16[1024,128]{1,0:T(8,128)(2,1)S(1)}, u32[]{:S(2)}, u32[]{:S(2)}) %collective-permute-start.2) | collective-permute-done | bytes 262176 | tf_op jit(solution)/shard_map/ppermute | solution.py:106
  24.2 6.0 %collective-permute-done.1 = bf16[1024,128]{1,0:T(8,128)(2,1)S(1)} collective-permute-done((bf16[1024,128]{1,0:T(8,128)(2,1)S(1)}, bf16[1024,128]{1,0:T(8,128)(2,1)S(1)}, u32[]{:S(2)}, u32[]{:S(2)}) %collective-permute-start.1) | collective-permute-done | bytes 262176 | tf_op jit(solution)/shard_map/ppermute | solution.py:104
  30.3 1.7 gather_fusion
  32.1 27.5 %while.25 = (s32[]{:T(128)}, f32[5,128,64]{1,2,0:T(8,128)S(1)}, f32[5,128]{1,0:T(8,128)S(1)}, f32[5,128]{1,0:T(8,128)S(1)}, f32[64,384]{1,0:T(8,128)S(1)}, /*ind...) while((s32[]{:T(128)}, f32[5,128,64]{1,2,0:T(8,128)S(1)}, ...), condition=%wide.region_12.14_spmd.clone, body=%wide.region_3.13_spmd.clone.sunk | while | flops 86640432 | bytes 7622712 | solution.py:147
  32.1 1.0 bitcast_reduce_fusion.4
  33.2 0.2 dynamic_update_slice.19
  33.4 0.6 dynamic_slice.37
  35.3 2.2 %conditional.3 = ((f32[5,128,64]{1,2,0:T(8,128)S(1)}, f32[5,128]{1,0:T(8,128)S(1)}, f32[5,128]{1,0:T(8,128)S(1)})) conditional(s32[]{:T(128)} %convert_element_type.31, (f32[5,128,64]{1,2,0:T(8,128)S(1)}, f32[5,128]{1,0:T(8,128)S(1)}, f32[5,128]{1,0:T(8,128)S(1)}) %tuple.78, (s32[]{:T(128)}, s32[128]{0:T(128)S(1)}, s32[64]{0:T(128)S(1)}, ...), branch_computations={%region_4.5_spmd, %region_5.9_spmd} | conditional | flops 86373136 | bytes 7155020 | solution.py:144
  35.8 0.4 fusion.25
  36.3 0.4 select_reduce_fusion
  36.7 0.4 copy.26
  37.5 0.9 bitcast_reduce_fusion.4
  38.5 0.2 dynamic_update_slice.19
  38.7 0.6 dynamic_slice.37
  40.6 0.9 bitcast_reduce_fusion.4
  41.7 0.2 dynamic_update_slice.19
  41.9 0.6 dynamic_slice.37
  43.8 0.9 bitcast_reduce_fusion.4
  45.1 0.6 dynamic_slice.37
  47.0 0.9 bitcast_reduce_fusion.4
  48.0 0.2 dynamic_update_slice.19
  48.2 0.6 dynamic_slice.37
  50.1 0.9 bitcast_reduce_fusion.4
  51.4 0.6 dynamic_slice.37
  53.3 0.9 bitcast_reduce_fusion.4
  54.6 0.6 dynamic_slice.37
  56.5 0.9 bitcast_reduce_fusion.4
  57.7 0.6 dynamic_slice.37
  60.1 0.2 convolution_bitcast_fusion.1
  60.3 0.2 fusion.4
  60.4 0.2 fusion.10
  60.6 0.3 convolution_bitcast_fusion
  61.0 0.2 fusion.23
  61.2 1.2 fusion.26
  62.4 1.4 fusion.8
  63.8 136.5 %all-reduce.3.cloned.1.call-done = (f32[5,128,128]{2,1,0:T(8,128)}, f32[384,128]{1,0:T(8,128)}) async-done(((f32[5,128,128]{2,1,0:T(8,128)}, f32[384,128]{1,0:T(8,128)}), (f32[5,128,128]{2,1,0:T(8,128)}, f32[384,128]{1,0:T(8,128)})) %all-reduce.3.cloned.1.call-update) | async-done | bytes 524304 | tf_op jit(solution)/shard_map/psum | solution.py:198
  200.3 1.7 copy.70
  202.0 1.6 copy.71
  (93 shorter events, 3.1 us)
Async XLA Ops:
  7.2 14.6 %copy-start = (bf16[5,128,128]{2,1,0:T(8,128)(2,1)S(1)}, bf16[5,128,128]{2,1,0:T(8,128)(2,1)}, u32[]{:S(2)}) copy-start(bf16[5,128,128]{2,1,0:T(8,128)(2,1)} %param.14) | copy-start | bytes 491524
  7.2 23.0 %copy-start.3 = (bf16[1024,128]{1,0:T(8,128)(2,1)S(1)}, bf16[1024,128]{1,0:T(8,128)(2,1)}, u32[]{:S(2)}) copy-start(bf16[1024,128]{1,0:T(8,128)(2,1)} %param.12) | copy-start | bytes 786436
  7.2 193.1 %all-reduce.3.cloned.1.call-start = ((), (), s32[]{:S(2)}) async-start(), calls=%async_computation | async-start | bytes 1048576 | tf_op jit(solution)/shard_map/psum | solution.py:198
  7.2 12.5 %collective-permute-start = (bf16[1024,128]{1,0:T(8,128)(2,1)}, bf16[1024,128]{1,0:T(8,128)(2,1)S(1)}, u32[]{:S(2)}, u32[]{:S(2)}) collective-permute-start(bf16[1024,128]{1,0:T(8,128)(2,1)} %param.12), channel_id=1, source_target_pairs={{0,1},{1,2},{2,3},{3,0},{4,5},{5,6},{6,7},{7,4},{8,9},{9,10},{10,1... | collective-permute-start | bytes 786440 | tf_op jit(solution)/shard_map/ppermute | solution.py:104
  10.3 13.8 %collective-permute-start.2 = (bf16[1024,128]{1,0:T(8,128)(2,1)}, bf16[1024,128]{1,0:T(8,128)(2,1)S(1)}, u32[]{:S(2)}, u32[]{:S(2)}) collective-permute-start(bf16[1024,128]{1,0:T(8,128)(2,1)} %param.12), channel_id=1, source_target_pairs={{1,0},{2,1},{3,2},{0,3},{5,4},{6,5},{7,6},{4,7},{9,8},{10,9},{11,1... | collective-permute-start | bytes 786440 | tf_op jit(solution)/shard_map/ppermute | solution.py:106
  19.8 10.4 %collective-permute-start.1 = (bf16[1024,128]{1,0:T(8,128)(2,1)S(1)}, bf16[1024,128]{1,0:T(8,128)(2,1)S(1)}, u32[]{:S(2)}, u32[]{:S(2)}) collective-permute-start(bf16[1024,128]{1,0:T(8,128)(2,1)S(1)} %collective-permute-done), channel_id=1, source_target_pairs={{0,1},{1,2},{2,3},{3,0},{4,5},{5,6},{6,7},{7,4},{8,9},{9,10},{10,1... | collective-permute-start | bytes 786440 | tf_op jit(solution)/shard_map/ppermute | solution.py:104
  30.3 1.7 copy-start.1
  30.3 1.7 copy-start.2
  32.1 28.0 %copy-start.4 = (bf16[384,128]{1,0:T(8,128)(2,1)S(1)}, bf16[384,128]{1,0:T(8,128)(2,1)}, u32[]{:S(2)}) copy-start(bf16[384,128]{1,0:T(8,128)(2,1)} %param.15) | copy-start | bytes 294916
  59.9 143.8 %copy-start.5 = (f32[5,2,64]{2,1,0:T(2,128)}, f32[5,2,64]{2,1,0:T(2,128)S(1)}, u32[]{:S(2)}) copy-start(f32[5,2,64]{2,1,0:T(2,128)S(1)} %bitcast_reduce_fusion.2) | copy-start | bytes 7684
Sparse Core Ops, SparseCore 0:
  63.9 136.3 all-reduce.2
